TPU v7x, 256 devices: a whole 4x4x8 slice. The times are simulated.
256 devices in a mesh: seq: 32 (over y, z), tensor: 8 (over x, core).
Axes of the slice: x: 4, y: 4, z: 8, core: 2. Of those that a mesh axis runs over, the one named last changes fastest.
Arguments:
- state: bfloat16 [32768, 2048], P('seq', 'tensor'), may hold values from -20.5 to 20.5
- memory: bfloat16 [512, 2048], P('seq', 'tensor'), may hold values from -20.5 to 20.5
- w_query: bfloat16 [2048, 2048], P('seq', 'tensor'), may hold values from -0.1875 to 0.1875
- w_key: bfloat16 [2048, 2048], P('seq', 'tensor'), may hold values from -0.1875 to 0.1875
- w_value: bfloat16 [2048, 2048], P('seq', 'tensor'), may hold values from -0.125 to 0.125
- w_output: bfloat16 [2048, 2048], P('tensor', 'seq'), may hold values from -0.375 to 0.375
- norm_gain: float32 [2048], P('tensor'), may hold values from 0.1 to 1.9
- remaining: int32 [32768], P('seq'), may hold values from 0 to 3
- slot_home: int32 [512], replicated, may hold values from 0 to 31
Outputs:
- new_state: bfloat16 [32768, 2048], P('seq', 'tensor')
- new_memory: bfloat16 [512, 2048], P('seq', 'tensor')
Inputs may be any that keep to these rules, and one draw needn't show every extreme that they name: `remaining`: 0 means the token has halted.
All inputs are finite; a program needn't handle non-finite values.
Results may differ from a plain program's by a relative error of at most 0.014.
The roundings to bfloat16 on the way count: a program that leaves them out, or rounds other values in their place, can miss the bound.
Values may be sent and summed in bfloat16 or wider, within the bound.
No kernel may reach another device: no remote copies, remote signals or barrier semaphores. Data moves between devices by JAX's collectives and lax.ppermute only.
A program may use at most 128 MiB of HBM per device.

v0:
```python
import math
import jax
import jax.numpy as jnp
from jax import lax
from jax.sharding import PartitionSpec as P

D = 2048
H = 16
HD = 128
HALF = 256
QB = 512
EPS = 1e-05
MASKED = -1e30


def with_halo(array, sides, width):
    for axis, dim in sides:
        peers, length = (lax.axis_size(axis), array.shape[dim])
        up = [(i, (i + 1) % peers) for i in range(peers - 1)]
        down = [(j, i) for i, j in up]
        last = lax.slice_in_dim(array, length - width, length, axis=dim)
        initial = lax.slice_in_dim(array, 0, width, axis=dim)
        before = lax.ppermute(last, axis, up)
        after = lax.ppermute(initial, axis, down)
        array = jnp.concatenate([before, array, after], axis=dim)
    return array


def merged(part, axis, combine):
    gathered = jax.tree.map(lambda a: lax.all_gather(a, axis), part)

    def take(source):
        return jax.tree.map(lambda a: lax.dynamic_index_in_dim(a, source, 0, False), gathered)

    return lax.fori_loop(
        1, lax.axis_size(axis), lambda source, state: combine(state, take(source)), take(0)
    )


def head_slopes(first, amount):
    order = (first + jnp.arange(amount, dtype=jnp.int32)).astype(jnp.float32)
    return 0.25 * 8.0 ** (order / (H - 1))


def shards(state, memory, w_query, w_key, w_value, w_output, norm_gain, remaining, slot_home):
    tok_rows = state.shape[0]
    slot_rows = memory.shape[0]
    seq_count = lax.axis_size("seq")
    seq_place = lax.axis_index("seq")
    tensor_place = lax.axis_index("tensor")
    local_width = w_query.shape[1]
    local_heads = local_width // HD
    total_tokens = tok_rows * seq_count
    score_scale = 1.0 / math.sqrt(HD)
    distance_slopes = head_slopes(tensor_place * local_heads, local_heads)
    homes = slot_home.astype(jnp.float32)
    home_gap = jnp.abs(homes - seq_place.astype(jnp.float32))
    slot_bias = distance_slopes[:, None] * home_gap[None, :]
    state_full, memory_full = (
        lax.all_gather(state, "tensor", axis=1, tiled=True),
        lax.all_gather(memory, "tensor", axis=1, tiled=True),
    )
    rows_full = jnp.concatenate([state_full, memory_full], axis=0)
    pieces = (
        lax.all_gather(w_query, "seq", axis=0, tiled=True),
        lax.all_gather(w_key, "seq", axis=0, tiled=True),
        lax.all_gather(w_value, "seq", axis=0, tiled=True),
    )
    query_acc, key_acc, value_acc = tuple(
        (jnp.dot(rows_full, piece, preferred_element_type=jnp.float32) for piece in pieces)
    )
    query = query_acc.astype(jnp.bfloat16)
    keys = key_acc.astype(jnp.bfloat16)
    values = value_acc.astype(jnp.bfloat16)
    slot_heads = jnp.concatenate([query[tok_rows:], keys[tok_rows:], values[tok_rows:]], axis=1)
    all_slots = lax.all_gather(slot_heads, "seq", axis=0, tiled=True)
    memory_slot_query = all_slots[:, :local_width].reshape(-1, local_heads, HD)
    memory_slot_keys = all_slots[:, local_width : 2 * local_width].reshape(-1, local_heads, HD)
    memory_slot_values = all_slots[:, 2 * local_width :].reshape(-1, local_heads, HD)
    token_key_rows = keys[:tok_rows].reshape(tok_rows, local_heads, HD)
    token_value_rows = values[:tok_rows].reshape(tok_rows, local_heads, HD)
    keys_values = jnp.concatenate([keys[:tok_rows], values[:tok_rows]], axis=1)
    padded = with_halo(keys_values, (("seq", 0),), HALF)
    block = QB
    window_extent = block + 2 * HALF

    def one_block(number):
        start = number * block
        query_matrix = lax.dynamic_slice_in_dim(query, start, block, 0).reshape(
            block, local_heads, HD
        )
        near_rows = lax.dynamic_slice_in_dim(padded, start, window_extent, 0)
        near_keys = near_rows[:, :local_width].reshape(window_extent, local_heads, HD)
        near_values = near_rows[:, local_width:].reshape(window_extent, local_heads, HD)
        near = (
            jnp.einsum("qhd,khd->hqk", query_matrix, near_keys, preferred_element_type=jnp.float32)
            * score_scale
        )
        first = seq_place * tok_rows + start
        qpos = first + jnp.arange(block, dtype=jnp.int32)
        kpos = first - HALF + jnp.arange(window_extent, dtype=jnp.int32)
        valid = (
            (jnp.abs(qpos[:, None] - kpos[None, :]) <= HALF)
            & (kpos >= 0)[None, :]
            & (kpos < total_tokens)[None, :]
        )
        near = jnp.where(valid[None], near, MASKED)
        distant_mask = (
            jnp.einsum(
                "taw,caw->atc", query_matrix, memory_slot_keys, preferred_element_type=jnp.float32
            )
            * score_scale
            - slot_bias[:, None, :]
        )
        scores = jnp.concatenate([near, distant_mask], axis=2)
        top = jnp.max(scores, axis=2, keepdims=True)
        exponent_terms = jnp.exp(scores - top)
        total = jnp.sum(exponent_terms, axis=2)
        attention_probabilities = exponent_terms.astype(jnp.bfloat16)
        numer = jnp.einsum(
            "hqk,khd->qhd",
            attention_probabilities[:, :, :window_extent],
            near_values,
            preferred_element_type=jnp.float32,
        )
        numer = numer + jnp.einsum(
            "lse,elf->slf",
            attention_probabilities[:, :, window_extent:],
            memory_slot_values,
            preferred_element_type=jnp.float32,
        )
        return (
            (numer / jnp.transpose(total)[:, :, None])
            .astype(jnp.bfloat16)
            .reshape(block, local_width)
        )

    token_mix = lax.map(one_block, jnp.arange(tok_rows // block, dtype=jnp.int32)).reshape(
        tok_rows, local_width
    )
    unnormalized_scores = (
        jnp.einsum(
            "gki,pki->kgp", memory_slot_query, token_key_rows, preferred_element_type=jnp.float32
        )
        * score_scale
        - slot_bias[:, :, None]
    )
    local_top = jnp.max(unnormalized_scores, axis=2)
    exponent_terms = jnp.exp(unnormalized_scores - local_top[:, :, None])
    local_sum = jnp.transpose(jnp.sum(exponent_terms, axis=2))
    local_num = jnp.einsum(
        "xzg,gxw->zxw",
        exponent_terms.astype(jnp.bfloat16),
        token_value_rows,
        preferred_element_type=jnp.float32,
    )
    local_top = jnp.transpose(local_top)

    def combine(first_part, second_part):
        top = jnp.maximum(first_part[0], second_part[0])
        weight_first = jnp.exp(first_part[0] - top)
        weight_second = jnp.exp(second_part[0] - top)
        sums = weight_first * first_part[1] + weight_second * second_part[1]
        numers = (
            weight_first[:, :, None] * first_part[2] + weight_second[:, :, None] * second_part[2]
        )
        return (top, sums, numers)

    merged_parts = merged((local_top, local_sum, local_num), "seq", combine)
    own_sum = lax.dynamic_slice_in_dim(merged_parts[1], seq_place * slot_rows, slot_rows, 0)
    own_num = lax.dynamic_slice_in_dim(merged_parts[2], seq_place * slot_rows, slot_rows, 0)
    slot_mix = (own_num / own_sum[:, :, None]).astype(jnp.bfloat16).reshape(slot_rows, local_width)
    mixed = jnp.concatenate([token_mix, slot_mix], axis=0)
    partial_rows = jnp.dot(
        mixed,
        lax.all_gather(w_output, "seq", axis=1, tiled=True),
        preferred_element_type=jnp.float32,
    )
    summed = lax.psum_scatter(
        partial_rows.astype(jnp.bfloat16), "tensor", scatter_dimension=1, tiled=True
    ).astype(jnp.float32)
    residual = jnp.concatenate([state, memory], axis=0).astype(jnp.float32) + summed
    squares = lax.psum(jnp.sum(residual * residual, axis=1), "tensor")
    normed_rows = (residual * lax.rsqrt(squares / D + EPS)[:, None] * norm_gain[None, :]).astype(
        jnp.bfloat16
    )
    new_state = jnp.where((remaining > 0)[:, None], normed_rows[:tok_rows], state)
    new_memory = normed_rows[tok_rows:]
    return (new_state, new_memory)


def solution(mesh):
    placed = (
        P("seq", "tensor"),
        P("seq", "tensor"),
        P("seq", "tensor"),
        P("seq", "tensor"),
        P("seq", "tensor"),
        P("tensor", "seq"),
        P("tensor"),
        P("seq"),
        P(),
    )
    return jax.shard_map(
        shards,
        mesh=mesh,
        in_specs=placed,
        out_specs=(P("seq", "tensor"), P("seq", "tensor")),
        check_vma=False,
    )
```

profile of v0, /device:TPU:1, one launch (start us, length us, event | category | flops | bytes accessed | tf_op | source)
XLA Modules:
  0.0 714.2 jit_solution(8940133622111685820)
XLA Ops:
  10.7 16.0 %all_gather.40 = bf16[16,2048]{1,0:T(8,128)(2,1)S(1)} all-gather(bf16[16,256]{1,0:T(8,128)(2,1)} %param.14), channel_id=1, replica_groups=mesh['seq'=32,'tensor'=8] {'tensor'}, dimensions={1}, use_global_device_ids=true | all-gather | bytes 73728 | tf_op jit(solution)/shard_map/all_gather | solution.py:61
  26.8 25.3 %all-gather.10.cloned.1.call-done = bf16[1024,2048]{1,0:T(8,128)(2,1)} async-done(((bf16[1024,256]{1,0:T(8,128)(2,1)}), bf16[1024,2048]{1,0:T(8,128)(2,1)}) %all-gather.10.cloned.1.call-update) | async-done | bytes 4194320 | tf_op jit(solution)/shard_map/all_gather | solution.py:60
  52.1 4.7 constant_dynamic-update-slice_fusion.2
  57.4 69.1 %all-gather.14.cloned.1.call-done = bf16[2048,256]{1,0:T(8,128)(2,1)} async-done(((bf16[64,256]{1,0:T(8,128)(2,1)}), bf16[2048,256]{1,0:T(8,128)(2,1)}) %all-gather.14.cloned.1.call-update) | async-done | bytes 1048592 | tf_op jit(solution)/shard_map/all_gather | solution.py:67
  126.5 3.8 convolution_convert_fusion.2
  130.4 72.6 %all-gather.12.cloned.1.call-done = bf16[2048,256]{1,0:T(8,128)(2,1)} async-done(((bf16[64,256]{1,0:T(8,128)(2,1)}), bf16[2048,256]{1,0:T(8,128)(2,1)}) %all-gather.12.cloned.1.call-update) | async-done | bytes 1048592 | tf_op jit(solution)/shard_map/all_gather | solution.py:66
  203.0 3.8 convolution_convert_fusion.3
  206.9 72.4 %all-gather.16.cloned.1.call-done = bf16[2048,256]{1,0:T(8,128)(2,1)} async-done(((bf16[64,256]{1,0:T(8,128)(2,1)}), bf16[2048,256]{1,0:T(8,128)(2,1)}) %all-gather.16.cloned.1.call-update) | async-done | bytes 1048592 | tf_op jit(solution)/shard_map/all_gather | solution.py:65
  279.3 3.8 convolution_convert_fusion.1
  284.1 36.9 %all_gather.44 = bf16[512,768]{1,0:T(8,128)(2,1)S(1)} all-gather(bf16[16,768]{1,0:T(8,128)(2,1)S(1)} %pad_maximum_fusion.4), channel_id=1, replica_groups=mesh['seq'=32,'tensor'=8] {'seq'}, dimensions={0}, use_global_device_ids=true | all-gather | bytes 811008 | tf_op jit(solution)/shard_map/all_gather | solution.py:76
  332.0 36.6 %all-gather = f32[16384,2]{0,1:T(2,128)S(1)} all-gather(f32[512,2]{0,1:T(2,128)S(1)} %bitcast.123), channel_id=2, replica_groups=mesh['seq'=32,'tensor'=8] {'seq'}, dimensions={0}, use_global_device_ids=true | all-gather | bytes 135168 | tf_op jit(solution)/shard_map/all_gather | solution.py:30
  371.9 35.7 %all-gather.1 = f32[16384,2]{0,1:T(2,128)S(1)} all-gather(f32[512,2]{0,1:T(2,128)S(1)} %bitcast.126), channel_id=3, replica_groups=mesh['seq'=32,'tensor'=8] {'seq'}, dimensions={0}, use_global_device_ids=true | all-gather | bytes 135168 | tf_op jit(solution)/shard_map/all_gather | solution.py:30
  409.9 22.6 %while.33 = (s32[]{:T(128)}, bf16[2,512,256]{2,1,0:T(8,128)(2,1)}, s32[2]{0:T(128)}, bf16[1536,512]{1,0:T(8,128)(2,1)S(1)}, s32[]{:T(128)}, /*index=5*/bf16[1040...) while((s32[]{:T(128)}, bf16[2,512,256]{2,1,0:T(8,128)(2,1)}, ...), condition=%wide.region_4.5_spmd.clone, body=%wide.region_0.4_spmd.clone.sunk | while | flops 819334656 | bytes 41282024 | solution.py:138
  432.4 48.4 %all-gather.20.cloned.1.call-done = f32[16384,2,128]{0,2,1:T(8,128)} async-done(((f32[512,2,128]{0,2,1:T(8,128)}), f32[16384,2,128]{0,2,1:T(8,128)}) %all-gather.20.cloned.1.call-update) | async-done | bytes 16777232 | tf_op jit(solution)/shard_map/all_gather | solution.py:30
  482.2 25.0 %copy.46 = f32[16384,2,128]{2,1,0:T(2,128)} copy(f32[16384,2,128]{0,2,1:T(8,128)} %all-gather.20.cloned.1.call-done) | data formatting | bytes 33554432 | tf_op jit(solution)/shard_map/while | solution.py:35
  507.1 140.4 %while.32 = (s32[]{:T(128)}, f32[512,2]{0,1:T(2,128)S(1)}, f32[512,2]{0,1:T(2,128)S(1)}, f32[512,2,128]{2,1,0:T(2,128)S(1)}, f32[32,512,2]{1,2,0:T(2,128)S(1)}, ...) while((s32[]{:T(128)}, f32[512,2]{0,1:T(2,128)S(1)}, ...), condition=%wide.region_8.9_spmd, body=%wide.region_7.8_spmd.sunk | while | flops 399365 | bytes 1630351 | solution.py:35
  508.2 3.5 fusion.77
  512.7 3.5 fusion.77
  517.3 3.5 fusion.77
  521.8 3.5 fusion.77
  526.3 3.5 fusion.77
  530.9 3.5 fusion.77
  535.4 3.5 fusion.77
  539.9 3.5 fusion.77
  544.5 3.5 fusion.77
  549.0 3.5 fusion.77
  553.5 3.5 fusion.77
  558.0 3.5 fusion.77
  562.5 3.5 fusion.77
  647.9 4.5 convolution_convert_fusion
  653.1 34.7 %reduce-scatter.2.cloned.1.call-done = bf16[1040,256]{1,0:T(8,128)(2,1)} async-done(((bf16[1040,2048]{1,0:T(8,128)(2,1)}), bf16[1040,256]{1,0:T(8,128)(2,1)}) %reduce-scatter.2.cloned.1.call-update) | async-done | bytes 532496 | tf_op jit(solution)/shard_map/reduce_scatter | solution.py:179
  689.1 15.3 %psum.7 = f32[1040]{0:T(1024)S(1)} all-reduce(f32[1040]{0:T(1024)S(1)} %multiply_reduce_fusion), channel_id=1, replica_groups=mesh['seq'=32,'tensor'=8] {'tensor'}, use_global_device_ids=true, to_apply=%region_11.12 | all-reduce | flops 1040 | bytes 8320 | tf_op jit(solution)/shard_map/psum | solution.py:183
  (249 shorter events, 143.0 us)
Async XLA Ops:
  7.2 44.9 %all-gather.10.cloned.1.call-start = ((), (), s32[]{:S(2)}) async-start(), calls=%async_computation.1 | async-start | bytes 4718592 | tf_op jit(solution)/shard_map/all_gather | solution.py:60
  7.9 118.6 %all-gather.14.cloned.1.call-start = ((), (), s32[]{:S(2)}) async-start(), calls=%async_computation.3 | async-start | bytes 1081344 | tf_op jit(solution)/shard_map/all_gather | solution.py:67
  8.6 194.4 %all-gather.12.cloned.1.call-start = ((), (), s32[]{:S(2)}) async-start(), calls=%async_computation.2 | async-start | bytes 1081344 | tf_op jit(solution)/shard_map/all_gather | solution.py:66
  9.4 270.0 %all-gather.16.cloned.1.call-start = ((), (), s32[]{:S(2)}) async-start(), calls=%async_computation.4 | async-start | bytes 1081344 | tf_op jit(solution)/shard_map/all_gather | solution.py:65
  10.0 470.9 %all-gather.20.cloned.1.call-start = ((), (), s32[]{:S(2)}) async-start(), calls=%async_computation.7 | async-start | bytes 17301504 | tf_op jit(solution)/shard_map/all_gather | solution.py:30
  10.7 46.1 %copy-start.11 = (f32[512]{0:T(512)}, f32[512]{0:T(512)S(1)}, u32[]{:S(2)}) copy-start(f32[512]{0:T(512)S(1)} %subtract_abs_fusion) | copy-start | bytes 6148
  26.7 30.1 %copy-start.14 = (f32[2]{0:T(128)}, f32[2]{0:T(128)S(1)}, u32[]{:S(2)}) copy-start(f32[2]{0:T(128)S(1)} %power_multiply_fusion) | copy-start | bytes 28
  26.8 295.1 %copy-start.13 = (f32[2,512]{1,0:T(2,128)}, f32[2,512]{1,0:T(2,128)S(1)}, u32[]{:S(2)}) copy-start(f32[2,512]{1,0:T(2,128)S(1)} %broadcast_multiply_fusion.1) | copy-start | bytes 12292
  284.1 39.7 %copy-start.8 = (bf16[1024,256]{0,1:T(8,128)(2,1)S(1)}, bf16[1024,256]{0,1:T(8,128)(2,1)}, u32[]{:S(2)}) copy-start(bf16[1024,256]{0,1:T(8,128)(2,1)} %copy.45) | copy-start | bytes 1572868
  321.9 1.9 copy-start
  325.9 322.0 %all-gather.18.cloned.1.call-start = ((), (), s32[]{:S(2)}) async-start(), calls=%async_computation.5 | async-start | bytes 1081344 | tf_op jit(solution)/shard_map/all_gather | solution.py:176
  326.5 361.3 %reduce-scatter.2.cloned.1.call-start = ((), (), s32[]{:S(2)}) async-start(), calls=%async_computation.6 | async-start | bytes 4792320 | tf_op jit(solution)/shard_map/reduce_scatter | solution.py:179
  326.6 81.1 %collective-permute-start = (bf16[256,512]{1,0:T(8,128)(2,1)S(1)}, bf16[256,512]{1,0:T(8,128)(2,1)S(1)}, u32[]{:S(2)}, u32[]{:S(2)}) collective-permute-start(bf16[256,512]{1,0:T(8,128)(2,1)S(1)} %get-tuple-element.403), channel_id=1, source_target_pairs={{0,8},{8,16},{16,24},{24,32},{32,40},{40,48},{48,56},{56,64},{64,7... | collective-permute-start | bytes 786440 | tf_op jit(solution)/shard_map/ppermute | solution.py:23
  329.1 79.2 %collective-permute-start.1 = (bf16[256,512]{1,0:T(8,128)(2,1)S(1)}, bf16[256,512]{1,0:T(8,128)(2,1)}, u32[]{:S(2)}, u32[]{:S(2)}) collective-permute-start(bf16[256,512]{1,0:T(8,128)(2,1)S(1)} %get-tuple-element.404), channel_id=1, source_target_pairs={{8,0},{16,8},{24,16},{32,24},{40,32},{48,40},{56,48},{64,56},{72,6... | collective-permute-start | bytes 786440 | tf_op jit(solution)/shard_map/ppermute | solution.py:24
  407.6 0.7 copy-start.10
  409.9 2.9 copy-start.3
  417.5 1.3 copy-start.1
  417.6 2.1 copy-start.9
  418.8 1.5 copy-start.5
  418.8 2.3 copy-start.4
  420.3 0.8 copy-start.6
  421.1 2.9 copy-start.3
  428.8 1.3 copy-start.1
  428.8 2.1 copy-start.9
  430.1 1.5 copy-start.5
  430.1 2.3 copy-start.4
  431.6 0.8 copy-start.6
  507.1 140.7 %copy-start.7 = (bf16[2,512,256]{2,1,0:T(8,128)(2,1)S(1)}, bf16[2,512,256]{2,1,0:T(8,128)(2,1)}, u32[]{:S(2)}) copy-start(bf16[2,512,256]{2,1,0:T(8,128)(2,1)} %get-tuple-element.294) | copy-start | bytes 1572868
  652.4 0.7 copy-start.15
  652.4 35.4 %copy-start.2 = (bf16[1024,256]{1,0:T(8,128)(2,1)S(1)}, bf16[1024,256]{1,0:T(8,128)(2,1)}, u32[]{:S(2)}) copy-start(bf16[1024,256]{1,0:T(8,128)(2,1)} %param.13) | copy-start | bytes 1572868
  652.4 35.4 %copy-start.12 = (bf16[16,256]{1,0:T(8,128)(2,1)S(1)}, bf16[16,256]{1,0:T(8,128)(2,1)}, u32[]{:S(2)}) copy-start(bf16[16,256]{1,0:T(8,128)(2,1)} %param.14) | copy-start | bytes 24580
  652.4 52.0 %copy-start.16 = (f32[256]{0:T(256)S(1)}, f32[256]{0:T(256)}, u32[]{:S(2)}) copy-start(f32[256]{0:T(256)} %param.19) | copy-start | bytes 3076
Sparse Core Ops, SparseCore 0:
  9.8 42.2 all-gather.9
  54.7 71.8 all-gather.13
  129.1 73.8 all-gather.11
  205.5 73.8 all-gather.15
  326.0 154.7 all-gather.19
  483.3 68.5 all-gather.17
  652.5 35.1 reduce-scatter.1
where the time goes:
time: 718 us; the launch traced here: 714 us
  waiting for transfers between devices  326 us (45%)
  other arithmetic  144 us (20%)
  blocking collectives  141 us (20%)
  local copies, waits for them, and re-layouts  55.6 us (8%)
  matrix products  26.7 us (4%)
  between operations  14.4 us (2%)
    add x31, other arithmetic, combine(): weight_first[:, :, None] * first_part[2]  108 us
    all_gather x1, waiting for transfers between devices, shards(): lax.all_gather(w_key, 'seq', axis=0, tiled=True)  72.6 us
    all_gather x1, waiting for transfers between devices, shards(): lax.all_gather(w_query, 'seq', axis=0, tiled=True)  72.4 us
    all_gather x2, blocking collectives, merged(): gathered = jax.tree.map(lambda a: lax.all_gather(a, axis), part)  72.3 us
    all_gather x1, waiting for transfers between devices, shards(): lax.all_gather(w_value, 'seq', axis=0, tiled=True)  69.1 us
    all_gather x1, waiting for transfers between devices, merged(): gathered = jax.tree.map(lambda a: lax.all_gather(a, axis), part)  48.4 us
    all_gather x1, blocking collectives, shards(): all_slots = lax.all_gather(slot_heads, 'seq', axis=0, tiled=True)  36.9 us
    reduce_scatter x1, waiting for transfers between devices, shards(): lax.psum_scatter(partial_rows.astype(jnp.bfloat16), 'tensor', scatter_dim...  34.7 us
  transfers between devices with their start and end apart: 9, of which 6 were waited for; matrix products, arithmetic and copies ran while one was open for 29% of the time, Pallas kernels for 0%

commit v1 on v0

--- a/solution.py
+++ b/solution.py
@@ -11,6 +11,12 @@
 QB = 512
 EPS = 1e-05
 MASKED = -1e30
+
+
+def gather_from_all(x, axis, dim):
+    peers = lax.axis_size(axis)
+    repeats = [peers if d == dim else 1 for d in range(x.ndim)]
+    return lax.all_to_all(jnp.tile(x, repeats), axis, split_axis=dim, concat_axis=dim, tiled=True)
 
 
 def with_halo(array, sides, width):
@@ -64,7 +70,7 @@
     pieces = (
         lax.all_gather(w_query, "seq", axis=0, tiled=True),
         lax.all_gather(w_key, "seq", axis=0, tiled=True),
-        lax.all_gather(w_value, "seq", axis=0, tiled=True),
+        gather_from_all(w_value, "seq", 0),
     )
     query_acc, key_acc, value_acc = tuple(
         (jnp.dot(rows_full, piece, preferred_element_type=jnp.float32) for piece in pieces)

time: 718 us -> 642 us (0.89)
  waiting for transfers between devices: 326 us -> 238 us
  starting transfers between devices: 4.04 us -> 16 us
    all_gather x1 -> x0, waiting for transfers between devices: 69.1 us -> none  [shards(): lax.all_gather(w_value, 'seq', axis=0, tiled=True)]
    all_to_all x0 -> x1, starting transfers between devices: none -> 12 us  [gather_from_all(): lax.all_to_all(jnp.tile(x, repeats), axis, split_axis=dim, concat_axis=di...]
    all_gather x1, waiting for transfers between devices: 25.3 us -> 13.9 us  [shards(): lax.all_gather(state, 'tensor', axis=1, tiled=True)]
  transfers between devices with their start and end apart: 9 -> 9, of which waited for: 6 -> 5; matrix products, arithmetic and copies ran while one was open for 29% -> 32% of each run, Pallas kernels for 0% -> 0%
where the time goes in v1:
time: 642 us; the launch traced here: 638 us
  waiting for transfers between devices  238 us (37%)
  other arithmetic  144 us (22%)
  blocking collectives  139 us (22%)
  local copies, waits for them, and re-layouts  57.6 us (9%)
  matrix products  26.4 us (4%)
  starting transfers between devices  16 us (2%)
  between operations  14.4 us (2%)
    add x31, other arithmetic, combine(): weight_first[:, :, None] * first_part[2]  108 us
    all_gather x1, waiting for transfers between devices, shards(): lax.all_gather(w_query, 'seq', axis=0, tiled=True)  72.5 us
    all_gather x2, blocking collectives, merged(): gathered = jax.tree.map(lambda a: lax.all_gather(a, axis), part)  72.4 us
    all_gather x1, waiting for transfers between devices, shards(): lax.all_gather(w_key, 'seq', axis=0, tiled=True)  65.6 us
    all_gather x1, waiting for transfers between devices, merged(): gathered = jax.tree.map(lambda a: lax.all_gather(a, axis), part)  48.2 us
    all_gather x1, blocking collectives, shards(): all_slots = lax.all_gather(slot_heads, 'seq', axis=0, tiled=True)  36.9 us
    reduce_scatter x1, waiting for transfers between devices, shards(): lax.psum_scatter(partial_rows.astype(jnp.bfloat16), 'tensor', scatter_dim...  34.6 us
    while x2, local copies, waits for them, and re-layouts, merged(): lax.fori_loop(1, lax.axis_size(axis), lambda source, state: combine(state...  25.2 us
  transfers between devices with their start and end apart: 9, of which 5 were waited for; matrix products, arithmetic and copies ran while one was open for 32% of the time, Pallas kernels for 0%

profile of v1, /device:TPU:1, one launch (start us, length us, event | category | flops | bytes accessed | tf_op | source)
XLA Modules:
  0.0 637.9 jit_solution(959577427608948657)
XLA Ops:
  10.5 12.0 %all-to-all-start = ((bf16[32,64,256]{2,1,0:T(8,128)(2,1)}), bf16[32,64,256]{2,1,0:T(8,128)(2,1)S(1)}, u32[]{:S(2)}, u32[]{:S(2)}) async-start(bf16[32,64,256]{2,1,0:T(8,128)(2,1)} %tile.2), calls=%async_computation | async-start | bytes 2097152 | tf_op jit(solution)/shard_map/all_to_all | solution.py:19
  24.0 14.2 %all_gather.37 = bf16[16,2048]{1,0:T(8,128)(2,1)S(1)} all-gather(bf16[16,256]{1,0:T(8,128)(2,1)} %param.14), channel_id=1, replica_groups=mesh['seq'=32,'tensor'=8] {'tensor'}, dimensions={1}, use_global_device_ids=true | all-gather | bytes 73728 | tf_op jit(solution)/shard_map/all_gather | solution.py:67
  38.3 13.9 %all-gather.9.cloned.1.call-done = bf16[1024,2048]{1,0:T(8,128)(2,1)} async-done(((bf16[1024,256]{1,0:T(8,128)(2,1)}), bf16[1024,2048]{1,0:T(8,128)(2,1)}) %all-gather.9.cloned.1.call-update) | async-done | bytes 4194320 | tf_op jit(solution)/shard_map/all_gather | solution.py:66
  52.3 4.7 constant_dynamic-update-slice_fusion.2
  61.2 65.6 %all-gather.11.cloned.1.call-done = bf16[2048,256]{1,0:T(8,128)(2,1)} async-done(((bf16[64,256]{1,0:T(8,128)(2,1)}), bf16[2048,256]{1,0:T(8,128)(2,1)}) %all-gather.11.cloned.1.call-update) | async-done | bytes 1048592 | tf_op jit(solution)/shard_map/all_gather | solution.py:72
  126.7 3.8 convolution_convert_fusion.3
  130.6 72.5 %all-gather.13.cloned.1.call-done = bf16[2048,256]{1,0:T(8,128)(2,1)} async-done(((bf16[64,256]{1,0:T(8,128)(2,1)}), bf16[2048,256]{1,0:T(8,128)(2,1)}) %all-gather.13.cloned.1.call-update) | async-done | bytes 1048592 | tf_op jit(solution)/shard_map/all_gather | solution.py:71
  203.2 3.8 convolution_convert_fusion.1
  208.0 36.9 %all_gather.40 = bf16[512,768]{1,0:T(8,128)(2,1)S(1)} all-gather(bf16[16,768]{1,0:T(8,128)(2,1)S(1)} %pad_maximum_fusion.4), channel_id=1, replica_groups=mesh['seq'=32,'tensor'=8] {'seq'}, dimensions={0}, use_global_device_ids=true | all-gather | bytes 811008 | tf_op jit(solution)/shard_map/all_gather | solution.py:82
  255.8 36.7 %all-gather = f32[16384,2]{0,1:T(2,128)S(1)} all-gather(f32[512,2]{0,1:T(2,128)S(1)} %bitcast.125), channel_id=2, replica_groups=mesh['seq'=32,'tensor'=8] {'seq'}, dimensions={0}, use_global_device_ids=true | all-gather | bytes 135168 | tf_op jit(solution)/shard_map/all_gather | solution.py:36
  295.8 35.7 %all-gather.1 = f32[16384,2]{0,1:T(2,128)S(1)} all-gather(f32[512,2]{0,1:T(2,128)S(1)} %bitcast.128), channel_id=3, replica_groups=mesh['seq'=32,'tensor'=8] {'seq'}, dimensions={0}, use_global_device_ids=true | all-gather | bytes 135168 | tf_op jit(solution)/shard_map/all_gather | solution.py:36
  333.7 22.7 %while.33 = (s32[]{:T(128)}, bf16[2,512,256]{2,1,0:T(8,128)(2,1)}, s32[2]{0:T(128)}, bf16[1536,512]{1,0:T(8,128)(2,1)S(1)}, s32[]{:T(128)}, /*index=5*/bf16[1040...) while((s32[]{:T(128)}, bf16[2,512,256]{2,1,0:T(8,128)(2,1)}, ...), condition=%wide.region_4.5_spmd.clone, body=%wide.region_0.4_spmd.clone.sunk | while | flops 819334656 | bytes 41282024 | solution.py:144
  356.4 48.2 %all-gather.17.cloned.1.call-done = f32[16384,2,128]{0,2,1:T(8,128)} async-done(((f32[512,2,128]{0,2,1:T(8,128)}), f32[16384,2,128]{0,2,1:T(8,128)}) %all-gather.17.cloned.1.call-update) | async-done | bytes 16777232 | tf_op jit(solution)/shard_map/all_gather | solution.py:36
  406.0 25.0 %copy.46 = f32[16384,2,128]{2,1,0:T(2,128)} copy(f32[16384,2,128]{0,2,1:T(8,128)} %all-gather.17.cloned.1.call-done) | data formatting | bytes 33554432 | tf_op jit(solution)/shard_map/while | solution.py:41
  430.9 140.4 %while.32 = (s32[]{:T(128)}, f32[512,2]{0,1:T(2,128)S(1)}, f32[512,2]{0,1:T(2,128)S(1)}, f32[512,2,128]{2,1,0:T(2,128)S(1)}, f32[32,512,2]{1,2,0:T(2,128)S(1)}, ...) while((s32[]{:T(128)}, f32[512,2]{0,1:T(2,128)S(1)}, ...), condition=%wide.region_8.9_spmd, body=%wide.region_7.8_spmd.sunk | while | flops 399365 | bytes 1630351 | solution.py:41
  432.0 3.5 fusion.77
  436.5 3.5 fusion.77
  441.1 3.5 fusion.77
  445.6 3.5 fusion.77
  450.1 3.5 fusion.77
  454.6 3.5 fusion.77
  459.2 3.5 fusion.77
  463.7 3.5 fusion.77
  468.2 3.5 fusion.77
  472.8 3.5 fusion.77
  477.3 3.5 fusion.77
  481.8 3.5 fusion.77
  486.4 3.5 fusion.77
  490.9 3.5 fusion.77
  571.7 4.5 convolution_convert_fusion
  576.9 34.6 %reduce-scatter.2.cloned.1.call-done = bf16[1040,256]{1,0:T(8,128)(2,1)} async-done(((bf16[1040,2048]{1,0:T(8,128)(2,1)}), bf16[1040,256]{1,0:T(8,128)(2,1)}) %reduce-scatter.2.cloned.1.call-update) | async-done | bytes 532496 | tf_op jit(solution)/shard_map/reduce_scatter | solution.py:185
  612.8 15.4 %psum.7 = f32[1040]{0:T(1024)S(1)} all-reduce(f32[1040]{0:T(1024)S(1)} %multiply_reduce_fusion), channel_id=1, replica_groups=mesh['seq'=32,'tensor'=8] {'tensor'}, use_global_device_ids=true, to_apply=%region_11.12 | all-reduce | flops 1040 | bytes 8320 | tf_op jit(solution)/shard_map/psum | solution.py:189
  (249 shorter events, 144.4 us)
Async XLA Ops:
  7.2 45.1 %all-gather.9.cloned.1.call-start = ((), (), s32[]{:S(2)}) async-start(), calls=%async_computation.2 | async-start | bytes 4718592 | tf_op jit(solution)/shard_map/all_gather | solution.py:66
  7.9 118.8 %all-gather.11.cloned.1.call-start = ((), (), s32[]{:S(2)}) async-start(), calls=%async_computation.3 | async-start | bytes 1081344 | tf_op jit(solution)/shard_map/all_gather | solution.py:72
  10.5 47.1 %all-to-all-start = ((bf16[32,64,256]{2,1,0:T(8,128)(2,1)}), bf16[32,64,256]{2,1,0:T(8,128)(2,1)S(1)}, u32[]{:S(2)}, u32[]{:S(2)}) async-start(bf16[32,64,256]{2,1,0:T(8,128)(2,1)} %tile.2), calls=%async_computation | async-start | bytes 2097152 | tf_op jit(solution)/shard_map/all_to_all | solution.py:19
  22.5 180.7 %all-gather.13.cloned.1.call-start = ((), (), s32[]{:S(2)}) async-start(), calls=%async_computation.4 | async-start | bytes 1081344 | tf_op jit(solution)/shard_map/all_gather | solution.py:71
  23.3 381.4 %all-gather.17.cloned.1.call-start = ((), (), s32[]{:S(2)}) async-start(), calls=%async_computation.7 | async-start | bytes 17301504 | tf_op jit(solution)/shard_map/all_gather | solution.py:36
  24.0 33.0 %copy-start.11 = (f32[512]{0:T(512)}, f32[512]{0:T(512)S(1)}, u32[]{:S(2)}) copy-start(f32[512]{0:T(512)S(1)} %subtract_abs_fusion) | copy-start | bytes 6148
  38.3 18.7 %copy-start.14 = (f32[2]{0:T(128)}, f32[2]{0:T(128)S(1)}, u32[]{:S(2)}) copy-start(f32[2]{0:T(128)S(1)} %power_multiply_fusion) | copy-start | bytes 28
  38.3 207.4 %copy-start.13 = (f32[2,512]{1,0:T(2,128)}, f32[2,512]{1,0:T(2,128)S(1)}, u32[]{:S(2)}) copy-start(f32[2,512]{1,0:T(2,128)S(1)} %broadcast_multiply_fusion.1) | copy-start | bytes 12292
  208.0 39.7 %copy-start.8 = (bf16[1024,256]{0,1:T(8,128)(2,1)S(1)}, bf16[1024,256]{0,1:T(8,128)(2,1)}, u32[]{:S(2)}) copy-start(bf16[1024,256]{0,1:T(8,128)(2,1)} %copy.45) | copy-start | bytes 1572868
  245.8 2.0 copy-start
  249.8 321.9 %all-gather.15.cloned.1.call-start = ((), (), s32[]{:S(2)}) async-start(), calls=%async_computation.5 | async-start | bytes 1081344 | tf_op jit(solution)/shard_map/all_gather | solution.py:182
  250.4 361.1 %reduce-scatter.2.cloned.1.call-start = ((), (), s32[]{:S(2)}) async-start(), calls=%async_computation.6 | async-start | bytes 4792320 | tf_op jit(solution)/shard_map/reduce_scatter | solution.py:185
  250.5 81.0 %collective-permute-start = (bf16[256,512]{1,0:T(8,128)(2,1)S(1)}, bf16[256,512]{1,0:T(8,128)(2,1)S(1)}, u32[]{:S(2)}, u32[]{:S(2)}) collective-permute-start(bf16[256,512]{1,0:T(8,128)(2,1)S(1)} %get-tuple-element.403), channel_id=1, source_target_pairs={{0,8},{8,16},{16,24},{24,32},{32,40},{40,48},{48,56},{56,64},{64,7... | collective-permute-start | bytes 786440 | tf_op jit(solution)/shard_map/ppermute | solution.py:29
  252.9 79.2 %collective-permute-start.1 = (bf16[256,512]{1,0:T(8,128)(2,1)S(1)}, bf16[256,512]{1,0:T(8,128)(2,1)}, u32[]{:S(2)}, u32[]{:S(2)}) collective-permute-start(bf16[256,512]{1,0:T(8,128)(2,1)S(1)} %get-tuple-element.404), channel_id=1, source_target_pairs={{8,0},{16,8},{24,16},{32,24},{40,32},{48,40},{56,48},{64,56},{72,6... | collective-permute-start | bytes 786440 | tf_op jit(solution)/shard_map/ppermute | solution.py:30
  331.5 0.6 copy-start.10
  333.7 2.9 copy-start.3
  341.5 1.3 copy-start.1
  341.5 2.1 copy-start.9
  342.7 1.5 copy-start.5
  342.7 2.3 copy-start.4
  344.2 0.8 copy-start.6
  345.1 2.9 copy-start.3
  352.8 1.3 copy-start.1
  352.8 2.1 copy-start.9
  354.1 1.5 copy-start.5
  354.1 2.3 copy-start.4
  355.6 0.8 copy-start.6
  430.9 140.7 %copy-start.7 = (bf16[2,512,256]{2,1,0:T(8,128)(2,1)S(1)}, bf16[2,512,256]{2,1,0:T(8,128)(2,1)}, u32[]{:S(2)}) copy-start(bf16[2,512,256]{2,1,0:T(8,128)(2,1)} %get-tuple-element.294) | copy-start | bytes 1572868
  576.2 0.7 copy-start.15
  576.2 35.3 %copy-start.2 = (bf16[1024,256]{1,0:T(8,128)(2,1)S(1)}, bf16[1024,256]{1,0:T(8,128)(2,1)}, u32[]{:S(2)}) copy-start(bf16[1024,256]{1,0:T(8,128)(2,1)} %param.13) | copy-start | bytes 1572868
  576.2 35.3 %copy-start.12 = (bf16[16,256]{1,0:T(8,128)(2,1)S(1)}, bf16[16,256]{1,0:T(8,128)(2,1)}, u32[]{:S(2)}) copy-start(bf16[16,256]{1,0:T(8,128)(2,1)} %param.14) | copy-start | bytes 24580
  576.2 52.0 %copy-start.16 = (f32[256]{0:T(256)S(1)}, f32[256]{0:T(256)}, u32[]{:S(2)}) copy-start(f32[256]{0:T(256)} %param.19) | copy-start | bytes 3076
Sparse Core Ops, SparseCore 0:
  9.8 42.4 all-gather.8
  54.8 71.8 all-gather.10
  129.3 73.8 all-gather.12
  249.9 154.7 all-gather.16
  407.1 68.5 all-gather.14
  576.4 35.1 reduce-scatter.1
